TPU v7x, 256 devices: a whole 4x4x8 slice. The times are simulated.
256 devices in a mesh: dst: 32 (over y, z), src: 8 (over x, core).
Axes of the slice: x: 4, y: 4, z: 8, core: 2. Of those that a mesh axis runs over, the one named last changes fastest.
Arguments:
- features: bfloat16 [131072, 128], P(('src', 'dst')), may hold values from -64 to 64
- projection: bfloat16 [128, 256], replicated, may hold values from -1 to 1
- source_att: float32 [256], replicated, may hold values from -1.5 to 1.5
- target_att: float32 [256], replicated, may hold values from -1 to 1
- out_bias: float32 [256], replicated, may hold values from -3 to 3
- block_coords: int32 [32, 8, 2, 256], P('dst', 'src'), may hold values from 0 to 127, as said below
- block_words: int32 [32, 8, 256, 16, 128], P('dst', 'src'), may hold values from 0 to 255, as said below
- block_counts: int32 [32, 8], P('dst', 'src'), may hold values from 1 to 256, as said below
Outputs:
- result: bfloat16 [131072, 256], P(('dst', 'src'))
Inputs may be any that keep to these rules, and one draw needn't show every extreme that they name: `block_coords`: row entries are below 32 and column entries below 128; the (row, column) pairs of one device's slots are distinct. `block_counts`: at least one device has all 256 slots live. `block_words`: each word holds an 8-bit pattern.
All inputs are finite; a program needn't handle non-finite values.
Results may differ from a plain program's by a relative error of at most 0.019.
Values may be sent and summed in bfloat16 or wider, within the bound.
No kernel may reach another device: no remote copies, remote signals or barrier semaphores. Data moves between devices by JAX's collectives and lax.ppermute only.
A program may use at most 128 MiB of HBM per device.

v0:
```python
import math
import jax
import jax.numpy as jnp
from jax import lax
from jax.sharding import PartitionSpec as P

HEADS = 8
HEAD_DIM = 32


def from_root(block, axis, holder):
    block = jnp.where(lax.axis_index(axis) == holder, block, jnp.zeros_like(block))
    return lax.psum(block, axis)


def leaky_relu(inputs):
    return jnp.where(inputs > 0, inputs, 0.2 * inputs)


def unpack(packed):
    shifts = jnp.arange(8, dtype=jnp.int32)
    spread = jnp.right_shift(packed[..., :, None, :], shifts[:, None]) & 1
    leading = packed.shape[:-2]
    flattened = spread.reshape(leading + (128, 128))
    return jnp.swapaxes(flattened, -1, -2) > 0


def terms_of(projected, source_att, target_att):
    source_part = jnp.sum(
        (projected * source_att).reshape(projected.shape[0], HEADS, HEAD_DIM), axis=-1
    )
    target_part = jnp.sum(
        (projected * target_att).reshape(projected.shape[0], HEADS, HEAD_DIM), axis=-1
    )
    return jnp.concatenate([source_part, target_part], axis=1).T


def on_device(
    features, projection, source_att, target_att, out_bias, block_coords, block_words, block_counts
):
    dst_count = lax.axis_size("dst")
    src_count = lax.axis_size("src")
    group_ratio = dst_count // src_count
    dst_index = lax.axis_index("dst")
    src_index = lax.axis_index("src")
    root_index = dst_index // group_ratio
    own_rows = features.shape[0]
    rows_dst = own_rows * src_count
    feature_width = projection.shape[1]
    projected = jnp.dot(features, projection, preferred_element_type=jnp.float32)
    gathered, score_terms = (
        lax.all_gather(projected.astype(jnp.bfloat16), "dst", axis=0, tiled=True),
        lax.all_gather(
            terms_of(projected, source_att, target_att).astype(jnp.bfloat16),
            "dst",
            axis=1,
            tiled=True,
        ).astype(jnp.float32),
    )
    src_rows = gathered.shape[0]
    row_blocks = rows_dst // 128
    col_blocks = src_rows // 128
    offset = dst_index % group_ratio * rows_dst
    target_own = lax.dynamic_slice_in_dim(score_terms[HEADS:], offset, rows_dst, 1)
    target_rows = from_root(target_own.astype(jnp.bfloat16), "src", root_index).astype(
        target_own.dtype
    )
    target_blocks = target_rows.reshape(HEADS, row_blocks, 128).transpose(1, 0, 2)
    source_blocks = score_terms[:HEADS].reshape(HEADS, col_blocks, 128).transpose(1, 0, 2)
    value_blocks = gathered.reshape(col_blocks, 128, HEADS, HEAD_DIM)
    self_source = (
        lax.dynamic_slice_in_dim(score_terms[:HEADS], offset, rows_dst, 1)
        .reshape(HEADS, row_blocks, 128)
        .transpose(1, 0, 2)
    )
    self_score = leaky_relu(target_blocks + self_source)
    is_root = src_index == root_index
    coords = block_coords[0, 0]
    packed_words = block_words[0, 0]
    live_count = block_counts[0, 0]
    group_size = math.gcd(packed_words.shape[0], 16)
    steps_live = (live_count + group_size - 1) // group_size

    def group_scores(step_index):
        first_slot = step_index * group_size
        row_ids = lax.dynamic_slice_in_dim(coords[0], first_slot, group_size)
        col_ids = lax.dynamic_slice_in_dim(coords[1], first_slot, group_size)
        packed = lax.dynamic_slice_in_dim(packed_words, first_slot, group_size, 0)
        valid_slot = first_slot + jnp.arange(group_size, dtype=jnp.int32) < live_count
        edge_mask = unpack(packed) & valid_slot[:, None, None]
        scores = leaky_relu(
            target_blocks[row_ids][:, :, :, None] + source_blocks[col_ids][:, :, None, :]
        )
        return (row_ids, col_ids, edge_mask, scores)

    def max_step(step_index, maxima):
        row_ids, col_ids, edge_mask, scores = group_scores(step_index)
        block_max = jnp.max(jnp.where(edge_mask[:, None], scores, -jnp.inf), axis=3)
        return maxima.at[row_ids].max(block_max)

    maxima = lax.fori_loop(
        0, steps_live, max_step, jnp.full((row_blocks, HEADS, 128), -jnp.inf, jnp.float32)
    )
    maxima = jnp.where(is_root, jnp.maximum(maxima, self_score), maxima)
    maxima = lax.pmax(maxima.astype(jnp.bfloat16), "src").astype(maxima.dtype)

    def sum_step(step_index, carry_state):
        weighted, denominator = carry_state
        row_ids, col_ids, edge_mask, scores = group_scores(step_index)
        weight = jnp.where(edge_mask[:, None], jnp.exp(scores - maxima[row_ids][..., None]), 0.0)
        rounded = weight.astype(jnp.bfloat16)
        contrib = jnp.einsum(
            "ghab,gbhc->gahc", rounded, value_blocks[col_ids], preferred_element_type=jnp.float32
        )
        contrib = contrib.reshape(group_size, 128, feature_width)
        weighted = weighted.at[row_ids].add(contrib)
        denominator = denominator.at[row_ids].add(jnp.sum(weight, axis=3))
        return (weighted, denominator)

    start_state = (
        jnp.zeros((row_blocks, 128, feature_width), jnp.float32),
        jnp.zeros((row_blocks, HEADS, 128), jnp.float32),
    )
    weighted, denominator = lax.fori_loop(0, steps_live, sum_step, start_state)
    self_weight = jnp.where(is_root, jnp.exp(self_score - maxima), 0.0)
    denominator = denominator + self_weight
    self_values = lax.dynamic_slice_in_dim(gathered, offset, rows_dst, 0).reshape(
        row_blocks, 128, HEADS, HEAD_DIM
    )
    self_rounded = lax.optimization_barrier(self_weight.astype(jnp.bfloat16))
    self_part = self_rounded.astype(jnp.float32).transpose(0, 2, 1)[..., None] * self_values.astype(
        jnp.float32
    )
    weighted = weighted + self_part.reshape(row_blocks, 128, feature_width)
    weighted_rows = weighted.reshape(rows_dst, feature_width)
    denominator_rows = denominator.transpose(1, 0, 2).reshape(HEADS, rows_dst)
    weighted_own, denominator_own = (
        lax.psum_scatter(
            weighted_rows.astype(jnp.bfloat16), "src", scatter_dimension=0, tiled=True
        ).astype(jnp.float32),
        lax.psum_scatter(
            denominator_rows.astype(jnp.bfloat16), "src", scatter_dimension=1, tiled=True
        ).astype(jnp.float32),
    )
    mixed_rows = weighted_own.reshape(own_rows, HEADS, HEAD_DIM) / denominator_own.T[:, :, None]
    result = jax.nn.elu(mixed_rows.reshape(own_rows, feature_width) + out_bias)
    return result.astype(jnp.bfloat16)


def solution(mesh):
    placed = (
        P(("src", "dst"), None),
        P(),
        P(),
        P(),
        P(),
        P("dst", "src", None, None),
        P("dst", "src", None, None, None),
        P("dst", "src"),
    )
    return jax.shard_map(
        on_device, mesh=mesh, in_specs=placed, out_specs=P(("dst", "src"), None), check_vma=False
    )
```

profile of v0, /device:TPU:8, one launch (start us, length us, event | category | flops | bytes accessed | tf_op | source)
XLA Modules:
  0.0 1036.6 jit_solution(7176538615227413374)
XLA Ops:
  8.3 1.9 bitcast_reduce_fusion.1
  10.2 52.3 %all_gather.7 = bf16[16,16384]{1,0:T(8,128)(2,1)S(1)} all-gather(bf16[16,512]{1,0:T(8,128)(2,1)S(1)} %maximum_bitcast_fusion), channel_id=1, replica_groups=mesh['dst'=32,'src'=8] {'dst'}, dimensions={1}, use_global_device_ids=true | all-gather | bytes 540672 | tf_op jit(solution)/shard_map/all_gather | solution.py:53
  64.1 61.0 %all-reduce.3.cloned.1.call-done = bf16[32,8,128]{2,1,0:T(8,128)(2,1)} async-done(((bf16[32,8,128]{2,1,0:T(8,128)(2,1)}), bf16[32,8,128]{2,1,0:T(8,128)(2,1)}) %all-reduce.3.cloned.1.call-update) | async-done | bytes 65552 | tf_op jit(solution)/shard_map/psum | solution.py:13
  125.9 38.4 %while.22 = (s32[]{:T(128)}, f32[32,8,128]{2,1,0:T(8,128)S(1)}, s32[]{:T(128)}, s32[2,256]{1,0:T(2,128)S(1)}, s32[256,16,128]{2,1,0:T(8,128)}, /*index=5*/s32[]{...) while((s32[]{:T(128)}, f32[32,8,128]{2,1,0:T(8,128)S(1)}, ...), condition=%wide.region_6.7_spmd, body=%wide.region_3.6_spmd.sunk | while | flops 13633670 | bytes 2112275 | solution.py:101
  129.7 4.7 fusion.61
  139.3 4.7 fusion.61
  148.9 4.7 fusion.61
  153.6 1.1 scatter_fusion
  158.5 4.7 fusion.61
  165.7 175.4 %all-reduce.5.cloned.1.call-done = bf16[32,8,128]{2,1,0:T(8,128)(2,1)} async-done(((bf16[32,8,128]{2,1,0:T(8,128)(2,1)}), bf16[32,8,128]{2,1,0:T(8,128)(2,1)}) %all-reduce.5.cloned.1.call-update) | async-done | bytes 65552 | tf_op jit(solution)/shard_map/pmax | solution.py:105
  341.1 1.5 convert_element_type.61
  342.6 38.5 %all-gather.2.cloned.1.call-done = bf16[16384,256]{0,1:T(8,128)(2,1)} async-done(((bf16[512,256]{0,1:T(8,128)(2,1)}), bf16[16384,256]{0,1:T(8,128)(2,1)}) %all-gather.2.cloned.1.call-update) | async-done | bytes 8388624 | tf_op jit(solution)/shard_map/all_gather | solution.py:52
  381.1 9.2 copy.53
  390.2 24.4 %copy.47 = bf16[128,128,8,32]{3,2,1,0:T(8,128)(2,1)} copy(bf16[128,128,8,32]{1,0,3,2:T(8,128)(2,1)} %bitcast.136) | data formatting | bytes 16777216 | tf_op jit(solution)/shard_map/while | solution.py:124
  414.6 2.4 broadcast_in_dim.36
  417.0 134.6 %while.23 = (s32[]{:T(128)}, f32[32,128,256]{2,1,0:T(8,128)}, f32[32,8,128]{2,1,0:T(8,128)S(1)}, s32[]{:T(128)}, s32[2,256]{1,0:T(2,128)S(1)}, /*index=5*/bf16[1...) while((s32[]{:T(128)}, f32[32,128,256]{2,1,0:T(8,128)}, ...), condition=%wide.region_12.13_spmd, body=%wide.region_8.12_spmd.sunk | while | flops 165152896 | bytes 18496492 | solution.py:124
  417.3 1.5 gather_fusion.3
  419.9 4.9 gather_fusion.2
  427.3 8.3 fusion.67
  435.6 1.9 copy.64
  437.5 4.5 scatter_fusion.1
  442.0 7.6 fusion.68
  450.9 1.5 gather_fusion.3
  453.5 5.0 gather_fusion.2
  461.0 8.3 fusion.67
  469.2 1.9 copy.64
  471.2 4.6 scatter_fusion.1
  475.7 7.6 fusion.68
  484.6 1.5 gather_fusion.3
  487.2 4.9 gather_fusion.2
  494.6 8.3 fusion.67
  502.9 1.9 copy.64
  504.8 4.4 scatter_fusion.1
  509.3 7.6 fusion.68
  516.9 1.1 scatter_fusion.2
  518.1 1.5 gather_fusion.3
  520.8 4.9 gather_fusion.2
  528.1 8.3 fusion.67
  536.4 1.9 copy.64
  538.3 4.5 scatter_fusion.1
  542.9 7.6 fusion.68
  551.6 5.6 copy.49
  557.2 1.6 fusion.42
  558.9 3.6 fusion.35
  562.6 2.9 copy.50
  565.5 424.4 %reduce-scatter.5.cloned.1.call-done = bf16[8,512]{1,0:T(8,128)(2,1)} async-done(((bf16[8,4096]{1,0:T(8,128)(2,1)}), bf16[8,512]{1,0:T(8,128)(2,1)}) %reduce-scatter.5.cloned.1.call-update) | async-done | bytes 8208 | tf_op jit(solution)/shard_map/reduce_scatter | solution.py:141
  990.9 36.6 %reduce-scatter.3.cloned.1.call-done = bf16[512,256]{1,0:T(8,128)(2,1)} async-done(((bf16[4096,256]{1,0:T(8,128)(2,1)}), bf16[512,256]{1,0:T(8,128)(2,1)}) %reduce-scatter.3.cloned.1.call-update) | async-done | bytes 262160 | tf_op jit(solution)/shard_map/reduce_scatter | solution.py:138
  1027.5 1.9 fusion.37
  (140 shorter events, 40.9 us)
Async XLA Ops:
  7.4 0.9 copy-start
  7.4 118.6 %copy-start.5 = (s32[1,1,2,256]{3,2,1,0:T(2,128)S(1)}, s32[1,1,2,256]{3,2,1,0:T(2,128)}, u32[]{:S(2)}) copy-start(s32[1,1,2,256]{3,2,1,0:T(2,128)} %param.17) | copy-start | bytes 6148
  7.4 117.7 %all-reduce.3.cloned.1.call-start = ((), (), s32[]{:S(2)}) async-start(), calls=%async_computation.3 | async-start | bytes 131072 | tf_op jit(solution)/shard_map/psum | solution.py:13
  63.2 277.9 %all-reduce.5.cloned.1.call-start = ((), (), s32[]{:S(2)}) async-start(), calls=%async_computation.4 | async-start | bytes 131072 | tf_op jit(solution)/shard_map/pmax | solution.py:105
  64.1 100.3 %copy-start.2 = (f32[8,16384]{1,0:T(8,128)}, f32[8,16384]{1,0:T(8,128)S(1)}, u32[]{:S(2)}) copy-start(f32[8,16384]{1,0:T(8,128)S(1)} %slice.34) | copy-start | bytes 1572868
  125.9 38.4 %copy-start.3 = (bf16[32,8,128]{2,1,0:T(8,128)(2,1)S(1)}, bf16[32,8,128]{2,1,0:T(8,128)(2,1)}, u32[]{:S(2)}) copy-start(bf16[32,8,128]{2,1,0:T(8,128)(2,1)} %all-reduce.3.cloned.1.call-done) | copy-start | bytes 196612
  165.1 216.0 %all-gather.2.cloned.1.call-start = ((), (), s32[]{:S(2)}) async-start(), calls=%async_computation.2 | async-start | bytes 8650752 | tf_op jit(solution)/shard_map/all_gather | solution.py:52
  165.6 824.3 %reduce-scatter.5.cloned.1.call-start = ((), (), s32[]{:S(2)}) async-start(), calls=%async_computation.6 | async-start | bytes 73728 | tf_op jit(solution)/shard_map/reduce_scatter | solution.py:141
  551.6 5.6 copy-start.4
  558.9 468.6 %reduce-scatter.3.cloned.1.call-start = ((), (), s32[]{:S(2)}) async-start(), calls=%async_computation.5 | async-start | bytes 2359296 | tf_op jit(solution)/shard_map/reduce_scatter | solution.py:138
  558.9 470.5 %copy-start.1 = (bf16[512,128]{1,0:T(8,128)(2,1)S(1)}, bf16[512,128]{1,0:T(8,128)(2,1)}, u32[]{:S(2)}) copy-start(bf16[512,128]{1,0:T(8,128)(2,1)} %param.12) | copy-start | bytes 393220
  562.6 464.9 %copy-start.6 = (f32[256]{0:T(256)S(1)}, f32[256]{0:T(256)}, u32[]{:S(2)}) copy-start(f32[256]{0:T(256)} %param.16) | copy-start | bytes 3076
Sparse Core Ops, SparseCore 0:
  63.3 61.7 all-reduce.2
  165.2 175.8 all-reduce.4
  559.0 430.9 reduce-scatter.4
  992.5 34.9 reduce-scatter.2
Sparse Core Ops, SparseCore 1:
  168.0 213.0 all-gather.1
where the time goes:
time: 1040 us
  waiting for transfers between devices  736 us (71%)
  local copies, waits for them, and re-layouts  99.6 us (10%)
  other arithmetic  96.5 us (9%)
  blocking collectives  52.3 us (5%)
  matrix products  35 us (3%)
  between operations  15.4 us (1%)
    reduce_scatter x1, waiting for transfers between devices, on_device(): lax.psum_scatter(denominator_rows.astype(jnp.bfloat16), 'src', scatter_di...  424 us
    pmax x1, waiting for transfers between devices, on_device(): maxima = lax.pmax(maxima.astype(jnp.bfloat16), 'src').astype(maxima.dtype)  175 us
    psum x1, waiting for transfers between devices, from_root(): return lax.psum(block, axis)  61 us
    all_gather x1, blocking collectives, on_device(): lax.all_gather(terms_of(projected, source_att, target_att).astype(jnp.bfl...  52.3 us
    all_gather x1, waiting for transfers between devices, on_device(): lax.all_gather(projected.astype(jnp.bfloat16), 'dst', axis=0, tiled=True)  38.5 us
    reduce_scatter x1, waiting for transfers between devices, on_device(): lax.psum_scatter(weighted_rows.astype(jnp.bfloat16), 'src', scatter_dimen...  36.6 us
    dot_general x4, matrix products, sum_step(): jnp.einsum('ghab,gbhc->gahc', rounded, value_blocks[col_ids], preferred_e...  33.1 us
    reduce_sum x4, other arithmetic, sum_step(): denominator = denominator.at[row_ids].add(jnp.sum(weight, axis=3))  30.6 us
  transfers between devices with their start and end apart: 5, of which 5 were waited for; matrix products, arithmetic and copies ran while one was open for 1% of the time, Pallas kernels for 0%

commit v1 on v0

--- a/solution.py
+++ b/solution.py
@@ -49,7 +49,12 @@
     feature_width = projection.shape[1]
     projected = jnp.dot(features, projection, preferred_element_type=jnp.float32)
     gathered, score_terms = (
-        lax.all_gather(projected.astype(jnp.bfloat16), "dst", axis=0, tiled=True),
+        jnp.concatenate(
+            lax.all_to_all(
+                jnp.stack([projected.astype(jnp.bfloat16)] * lax.axis_size("dst")), "dst", 0, 0
+            ),
+            axis=0,
+        ),
         lax.all_gather(
             terms_of(projected, source_att, target_att).astype(jnp.bfloat16),
             "dst",

time: 1040 us -> 1200 us (1.15)
  blocking collectives: 52.3 us -> 238 us
  waiting for transfers between devices: 736 us -> 678 us
  local copies, waits for them, and re-layouts: 99.6 us -> 120 us
    all_gather x1, blocking collectives: 52.3 us -> 238 us  [on_device(): lax.all_gather(terms_of(projected, source_att, target_att).astype(jnp.bfl...]
    all_gather x1 -> x0, waiting for transfers between devices: 38.5 us -> none  [on_device(): lax.all_gather(projected.astype(jnp.bfloat16), 'dst', axis=0, tiled=True)]
    while x2 -> x3, local copies, waits for them, and re-layouts: 30 us -> 53.5 us  [on_device(): weighted, denominator = lax.fori_loop(0, steps_live, sum_step, start_state)]
    reduce_scatter x1, waiting for transfers between devices: 424 us -> 407 us  [on_device(): lax.psum_scatter(denominator_rows.astype(jnp.bfloat16), 'src', scatter_di...]
  transfers between devices with their start and end apart: 5 -> 5, of which waited for: 5 -> 4; matrix products, arithmetic and copies ran while one was open for 1% -> 5% of each run, Pallas kernels for 0% -> 0%
where the time goes in v1:
time: 1200 us; the launch traced here: 1190 us
  waiting for transfers between devices  678 us (56%)
  blocking collectives  238 us (20%)
  local copies, waits for them, and re-layouts  120 us (10%)
  other arithmetic  96.8 us (8%)
  matrix products  34.3 us (3%)
  between operations  14 us (1%)
    reduce_scatter x1, waiting for transfers between devices, on_device(): lax.psum_scatter(denominator_rows.astype(jnp.bfloat16), 'src', scatter_di...  407 us
    all_gather x1, blocking collectives, on_device(): lax.all_gather(terms_of(projected, source_att, target_att).astype(jnp.bfl...  238 us
    pmax x1, waiting for transfers between devices, on_device(): maxima = lax.pmax(maxima.astype(jnp.bfloat16), 'src').astype(maxima.dtype)  175 us
    psum x1, waiting for transfers between devices, from_root(): return lax.psum(block, axis)  59.5 us
    while x3, local copies, waits for them, and re-layouts, on_device(): weighted, denominator = lax.fori_loop(0, steps_live, sum_step, start_state)  53.5 us
    reduce_scatter x1, waiting for transfers between devices, on_device(): lax.psum_scatter(weighted_rows.astype(jnp.bfloat16), 'src', scatter_dimen...  36.6 us
    dot_general x4, matrix products, sum_step(): jnp.einsum('ghab,gbhc->gahc', rounded, value_blocks[col_ids], preferred_e...  33.1 us
    reduce_sum x4, other arithmetic, sum_step(): denominator = denominator.at[row_ids].add(jnp.sum(weight, axis=3))  30.6 us
  transfers between devices with their start and end apart: 5, of which 4 were waited for; matrix products, arithmetic and copies ran while one was open for 5% of the time, Pallas kernels for 0%

profile of v1, /device:TPU:8, one launch (start us, length us, event | category | flops | bytes accessed | tf_op | source)
XLA Modules:
  0.0 1192.9 jit_solution(16041884827673842212)
XLA Ops:
  7.4 1.2 bitcast_reduce_fusion.1
  8.7 4.2 stack.2
  12.8 11.8 all-to-all-start
  24.7 237.8 %all_gather.3 = bf16[16,16384]{1,0:T(8,128)(2,1)S(1)} all-gather(bf16[16,512]{1,0:T(8,128)(2,1)S(1)} %maximum_bitcast_fusion), channel_id=1, replica_groups=mesh['dst'=32,'src'=8] {'dst'}, dimensions={1}, use_global_device_ids=true | all-gather | bytes 540672 | tf_op jit(solution)/shard_map/all_gather | solution.py:58
  264.1 59.5 %all-reduce.3.cloned.1.call-done = bf16[32,8,128]{2,1,0:T(8,128)(2,1)} async-done(((bf16[32,8,128]{2,1,0:T(8,128)(2,1)}), bf16[32,8,128]{2,1,0:T(8,128)(2,1)}) %all-reduce.3.cloned.1.call-update) | async-done | bytes 65552 | tf_op jit(solution)/shard_map/psum | solution.py:13
  324.5 38.4 %while.22 = (s32[]{:T(128)}, f32[32,8,128]{2,1,0:T(8,128)S(1)}, s32[]{:T(128)}, s32[2,256]{1,0:T(2,128)S(1)}, s32[256,16,128]{2,1,0:T(8,128)}, /*index=5*/s32[]{...) while((s32[]{:T(128)}, f32[32,8,128]{2,1,0:T(8,128)S(1)}, ...), condition=%wide.region_6.7_spmd, body=%wide.region_3.6_spmd.sunk | while | flops 13633670 | bytes 2112275 | solution.py:106
  328.2 4.7 fusion.61
  337.8 4.7 fusion.61
  347.4 4.7 fusion.61
  352.1 1.1 scatter_fusion
  357.0 4.7 fusion.61
  361.7 1.1 scatter_fusion
  363.6 174.9 %all-reduce.5.cloned.1.call-done = bf16[32,8,128]{2,1,0:T(8,128)(2,1)} async-done(((bf16[32,8,128]{2,1,0:T(8,128)(2,1)}), bf16[32,8,128]{2,1,0:T(8,128)(2,1)}) %all-reduce.5.cloned.1.call-update) | async-done | bytes 65552 | tf_op jit(solution)/shard_map/pmax | solution.py:110
  539.4 11.9 %copy.66 = bf16[32,512,256]{2,1,0:T(8,128)(2,1)} copy(bf16[32,512,256]{1,2,0:T(8,128)(2,1)} %all-to-all-done) | data formatting | bytes 16777216 | tf_op jit(solution)/shard_map/while | solution.py:129
  551.3 36.0 %reshape.262 = bf16[128,128,8,32]{3,2,1,0:T(8,128)(2,1)} reshape(bf16[32,512,256]{2,1,0:T(8,128)(2,1)} %copy.66) | data formatting | bytes 16777216 | tf_op jit(solution)/shard_map/while | solution.py:129
  587.3 1.7 constant_dynamic-slice_fusion.6
  589.0 3.4 copy.62
  592.4 2.4 broadcast_in_dim.36
  594.9 130.8 %while.23 = (s32[]{:T(128)}, f32[32,128,256]{2,1,0:T(8,128)}, f32[32,8,128]{2,1,0:T(8,128)S(1)}, s32[]{:T(128)}, s32[2,256]{1,0:T(2,128)S(1)}, /*index=5*/bf16[1...) while((s32[]{:T(128)}, f32[32,128,256]{2,1,0:T(8,128)}, ...), condition=%wide.region_12.13_spmd, body=%wide.region_8.12_spmd.sunk | while | flops 165152896 | bytes 18496492 | solution.py:129
  599.2 7.7 fusion.68
  606.9 1.1 scatter_fusion.2
  608.0 4.9 gather_fusion.2
  612.8 8.3 fusion.67
  621.1 1.9 copy.77
  623.0 4.5 scatter_fusion.1
  631.9 7.7 fusion.68
  640.6 5.0 gather_fusion.2
  645.6 8.3 fusion.67
  653.9 1.9 copy.77
  655.8 4.5 scatter_fusion.1
  664.6 7.7 fusion.68
  672.3 1.1 scatter_fusion.2
  673.4 4.9 gather_fusion.2
  678.3 8.3 fusion.67
  686.5 1.9 copy.77
  688.5 4.4 scatter_fusion.1
  697.2 7.7 fusion.68
  706.0 4.9 gather_fusion.2
  710.8 8.3 fusion.67
  719.1 1.9 copy.77
  721.0 4.6 scatter_fusion.1
  725.6 1.6 fusion.42
  727.3 5.6 copy.63
  732.9 4.5 fusion.35
  737.4 2.9 copy.64
  740.3 406.5 %reduce-scatter.5.cloned.1.call-done = bf16[8,512]{1,0:T(8,128)(2,1)} async-done(((bf16[8,4096]{1,0:T(8,128)(2,1)}), bf16[8,512]{1,0:T(8,128)(2,1)}) %reduce-scatter.5.cloned.1.call-update) | async-done | bytes 8208 | tf_op jit(solution)/shard_map/reduce_scatter | solution.py:146
  1147.8 36.6 %reduce-scatter.3.cloned.1.call-done = bf16[512,256]{1,0:T(8,128)(2,1)} async-done(((bf16[4096,256]{1,0:T(8,128)(2,1)}), bf16[512,256]{1,0:T(8,128)(2,1)}) %reduce-scatter.3.cloned.1.call-update) | async-done | bytes 262160 | tf_op jit(solution)/shard_map/reduce_scatter | solution.py:143
  1184.4 1.9 fusion.37
  (142 shorter events, 41.3 us)
Async XLA Ops:
  6.5 0.9 copy-start
  12.8 526.5 %all-to-all-start = ((bf16[32,512,256]{1,2,0:T(8,128)(2,1)}), bf16[32,512,256]{1,2,0:T(8,128)(2,1)}, u32[]{:S(2)}, u32[]{:S(2)}) async-start(bf16[32,512,256]{1,2,0:T(8,128)(2,1)} %stack.2), calls=%async_computation | async-start | bytes 16777216 | tf_op jit(solution)/shard_map/all_to_all | solution.py:53
  24.6 299.9 %copy-start.5 = (s32[1,1,2,256]{3,2,1,0:T(2,128)S(1)}, s32[1,1,2,256]{3,2,1,0:T(2,128)}, u32[]{:S(2)}) copy-start(s32[1,1,2,256]{3,2,1,0:T(2,128)} %param.17) | copy-start | bytes 6148
  24.6 299.0 %all-reduce.3.cloned.1.call-start = ((), (), s32[]{:S(2)}) async-start(), calls=%async_computation.3 | async-start | bytes 131072 | tf_op jit(solution)/shard_map/psum | solution.py:13
  263.2 275.3 %all-reduce.5.cloned.1.call-start = ((), (), s32[]{:S(2)}) async-start(), calls=%async_computation.4 | async-start | bytes 131072 | tf_op jit(solution)/shard_map/pmax | solution.py:110
  264.0 98.8 %copy-start.2 = (f32[8,16384]{1,0:T(8,128)}, f32[8,16384]{1,0:T(8,128)S(1)}, u32[]{:S(2)}) copy-start(f32[8,16384]{1,0:T(8,128)S(1)} %slice.34) | copy-start | bytes 1572868
  324.4 38.4 %copy-start.3 = (bf16[32,8,128]{2,1,0:T(8,128)(2,1)S(1)}, bf16[32,8,128]{2,1,0:T(8,128)(2,1)}, u32[]{:S(2)}) copy-start(bf16[32,8,128]{2,1,0:T(8,128)(2,1)} %all-reduce.3.cloned.1.call-done) | copy-start | bytes 196612
  363.5 783.3 %reduce-scatter.5.cloned.1.call-start = ((), (), s32[]{:S(2)}) async-start(), calls=%async_computation.6 | async-start | bytes 73728 | tf_op jit(solution)/shard_map/reduce_scatter | solution.py:146
  594.9 130.8 %copy-start.4 = (bf16[32,8,128]{2,1,0:T(8,128)(2,1)S(1)}, bf16[32,8,128]{2,1,0:T(8,128)(2,1)}, u32[]{:S(2)}) copy-start(bf16[32,8,128]{2,1,0:T(8,128)(2,1)} %all-reduce.5.cloned.1.call-done) | copy-start | bytes 196612
  727.3 457.1 %reduce-scatter.3.cloned.1.call-start = ((), (), s32[]{:S(2)}) async-start(), calls=%async_computation.5 | async-start | bytes 2359296 | tf_op jit(solution)/shard_map/reduce_scatter | solution.py:143
  732.9 453.4 %copy-start.1 = (bf16[512,128]{1,0:T(8,128)(2,1)S(1)}, bf16[512,128]{1,0:T(8,128)(2,1)}, u32[]{:S(2)}) copy-start(bf16[512,128]{1,0:T(8,128)(2,1)} %param.12) | copy-start | bytes 393220
  737.4 447.0 %copy-start.6 = (f32[256]{0:T(256)S(1)}, f32[256]{0:T(256)}, u32[]{:S(2)}) copy-start(f32[256]{0:T(256)} %param.16) | copy-start | bytes 3076
Sparse Core Ops, SparseCore 0:
  263.3 60.2 all-reduce.2
  363.7 174.7 all-reduce.4
  727.4 419.4 reduce-scatter.4
  1149.4 34.9 reduce-scatter.2
